TPU v7x, 256 devices: a whole 4x4x8 slice. The times are simulated.
256 devices in a mesh: col: 16 (over z, core), tile: 16 (over y, x).
Axes of the slice: x: 4, y: 4, z: 8, core: 2. Of those that a mesh axis runs over, the one named last changes fastest.
Arguments:
- boundary: bfloat16 [16, 1024, 4, 1024], P('col', 'tile'), may hold values from -6 to 6
- row_tensors: bfloat16 [16, 4, 4, 4, 4], P('col'), may hold values from -3 to 3
- sketch_bond: bfloat16 [16, 1024, 1024], P('col', 'tile'), may hold values from -0.1875 to 0.1875
- sketch_phys: bfloat16 [16, 4, 4, 1024], P('col'), may hold values from -6 to 6
- edge_factor: bfloat16 [1024, 4, 1024], P('tile'), may hold values from -0.09375 to 0.09375
- closing: float32 [16, 4], P('col'), may hold values from 0.2 to 2
- left_edge: float32 [1024], replicated, may hold values from -6 to 6
Outputs:
- new_boundary: bfloat16 [16, 1024, 4, 1024], P('col', 'tile')
- envs: float32 [16, 1024], P('col', 'tile')
All inputs are finite; a program needn't handle non-finite values.
Results may differ from a plain program's by a relative error of at most 0.012.
The roundings to bfloat16 on the way count: a program that leaves them out, or rounds other values in their place, can miss the bound.
Values may be sent and summed in bfloat16 or wider, within the bound.
A program may use at most 128 MiB of HBM per device.

v0:
```python
import jax
import jax.numpy as jnp
from jax import lax
from jax.sharding import PartitionSpec as P

GRAM_SHIFT = 0.001


def passed_along(block, axis, distance):
    devices = range(lax.axis_size(axis))
    route = [(i - distance, i) for i in devices if i - distance in devices]
    return lax.ppermute(block, axis, route)


def local(boundary, row_tensors, sketch_bond, sketch_phys, edge_factor, closing, left_edge):
    highest = lax.Precision.HIGHEST
    own_site = boundary[0]
    row_tensor = row_tensors[0].astype(jnp.float32)
    bond_sketch = sketch_bond[0]
    phys_map = jnp.einsum(
        "lurd,ldk->urk", row_tensor, sketch_phys[0].astype(jnp.float32), precision=highest
    )
    local_rows = own_site.shape[0]
    legs = own_site.shape[1]
    width = own_site.shape[2]
    sketched = jnp.einsum(
        "bua,ka->buk",
        own_site,
        lax.all_gather(bond_sketch, "tile", axis=0, tiled=True),
        preferred_element_type=jnp.float32,
    )
    range_rows = jnp.sum(sketched[:, :, None, :] * phys_map[None], axis=1)
    range_flat = range_rows.reshape(local_rows * legs, width)
    gram_local = jnp.dot(range_flat.T, range_flat, precision=highest)
    gram_total = lax.psum(gram_local, "tile") + GRAM_SHIFT * jnp.eye(width, dtype=jnp.float32)
    lower_factor = jnp.linalg.cholesky(gram_total)
    basis = jax.scipy.linalg.solve_triangular(lower_factor, range_flat.T, lower=True).T
    basis = basis.astype(jnp.bfloat16).reshape(local_rows, legs, width)
    arrived = passed_along(basis, "col", 1)
    first_column = lax.axis_index("col") == 0
    left_basis = jnp.where(first_column, edge_factor, arrived)
    matching = own_site
    left_part = jnp.einsum(
        "alc,bua->club",
        lax.all_gather(left_basis, "tile", axis=0, tiled=True),
        matching,
        preferred_element_type=jnp.float32,
    )
    left_absorbed = jnp.einsum("club,lurd->cdbr", left_part, row_tensor, precision=highest)
    matching = basis.astype(jnp.float32)
    new_site = lax.psum_scatter(
        jnp.einsum("cdbr,brk->kdc", left_absorbed, matching, precision=highest),
        "tile",
        scatter_dimension=0,
        tiled=True,
    )
    new_site = new_site.astype(jnp.bfloat16)
    transfer_rows = jnp.einsum(
        "kdc,d->kc", new_site.astype(jnp.float32), closing[0], precision=highest
    ).astype(jnp.bfloat16)
    scale = jnp.sqrt(jnp.float32(width))
    column_count = lax.axis_size("col")
    share = transfer_rows.shape[0]
    transfer_local = transfer_rows.astype(jnp.float32)

    def relay_split(turn_index, current):
        incoming = passed_along(current, "col", 1)
        incoming_whole = lax.all_gather(incoming, "tile", axis=0, tiled=True)
        incoming_whole = jnp.where(first_column, left_edge, incoming_whole)
        weighted = jnp.dot(transfer_local, incoming_whole, precision=highest)
        squares = lax.psum(jnp.sum(weighted * weighted), "tile")
        return weighted * scale / jnp.sqrt(squares + 1e-06)

    env_local = lax.fori_loop(0, column_count, relay_split, jnp.zeros((share,), jnp.float32))
    return (new_site[None], env_local[None])


def solution(mesh):
    in_specs = (
        P("col", "tile", None, None),
        P("col", None, None, None, None),
        P("col", "tile", None),
        P("col", None, None, None),
        P("tile", None, None),
        P("col", None),
        P(),
    )
    out_specs = (P("col", "tile", None, None), P("col", "tile"))
    return jax.shard_map(local, mesh=mesh, in_specs=in_specs, out_specs=out_specs, check_vma=False)
```

profile of v0, /device:TPU:130, one launch (start us, length us, event | category | flops | bytes accessed | tf_op | source)
XLA Modules:
  0.0 2074.5 jit_solution(1009974480985089670)
XLA Ops:
  9.1 52.4 %all-gather.6.cloned.1.call-done = bf16[1,1024,1024]{2,1,0:T(8,128)(2,1)} async-done(((bf16[1,64,1024]{2,1,0:T(8,128)(2,1)}), bf16[1,1024,1024]{2,1,0:T(8,128)(2,1)}) %all-gather.6.cloned.1.call-update) | async-done | bytes 2097168 | tf_op jit(solution)/shard_map/all_gather | solution.py:29
  71.0 112.0 %all-reduce.7.cloned.1.call-done = f32[1024,1024]{0,1:T(8,128)} async-done(((f32[1024,1024]{0,1:T(8,128)}), f32[1024,1024]{0,1:T(8,128)}) %all-reduce.7.cloned.1.call-update) | async-done | bytes 4194320 | tf_op jit(solution)/shard_map/psum | solution.py:35
  435.0 78.8 %custom-call.70 = f32[8,128,128]{1,2,0:T(8,128)S(1)} custom-call(f32[8,128,128]{2,1,0:T(8,128)S(1)} %get-tuple-element.37), custom_call_target="InvertDiagBlocksLowerTriangular" | custom-call | tf_op jit(solution)/shard_map/jit(_solve_triangular)/triangular_solve | solution.py:37
  540.9 75.5 %all-gather.4.cloned.1.call-done = bf16[1024,4,1024]{2,1,0:T(4,128)(2,1)} async-done(((bf16[64,4,1024]{2,1,0:T(4,128)(2,1)}), bf16[1024,4,1024]{2,1,0:T(4,128)(2,1)}) %all-gather.4.cloned.1.call-update) | async-done | bytes 8388624 | tf_op jit(solution)/shard_map/all_gather | solution.py:45
  642.2 115.3 %reduce-scatter.2.cloned.1.call-done = f32[64,4,1024]{2,0,1:T(8,128)} async-done(((f32[1024,4,1024]{2,0,1:T(8,128)}), f32[64,4,1024]{2,0,1:T(8,128)}) %reduce-scatter.2.cloned.1.call-update) | async-done | bytes 1048592 | tf_op jit(solution)/shard_map/reduce_scatter | solution.py:51
  762.4 1304.7 %while.13 = (s32[]{:T(128)}, f32[64]{0:T(128)S(1)}, pred[]{:T(512)}, f32[1024]{0:T(1024)S(1)}, f32[64,1024]{1,0:T(8,128)S(1)}, /*index=5*/s32[]{:T(128)}, f32[]{...) while((s32[]{:T(128)}, f32[64]{0:T(128)S(1)}, ...), condition=%wide.region_22.23_spmd.clone, body=%wide.region_19.22_spmd.clone.sunk | while | flops 788807 | bytes 293892 | solution.py:74
  768.7 36.4 %all-reduce.4 = f32[1024]{0:T(1024)S(1)} all-reduce(f32[1024]{0:T(1024)S(1)} %dynamic-update-slice.105), channel_id=1, replica_groups=mesh['col'=16,'tile'=16] {'tile'}, use_global_device_ids=true, to_apply=%add.1 | all-reduce | flops 1024 | bytes 8192 | tf_op jit(solution)/shard_map/while
  806.1 38.7 %psum.17 = f32[]{:T(128)} all-reduce(f32[]{:T(128)} %get-tuple-element.212), channel_id=1, replica_groups=mesh['col'=16,'tile'=16] {'tile'}, use_global_device_ids=true, to_apply=%region_21.21 | all-reduce | flops 1 | bytes 8 | tf_op jit(solution)/shard_map/while/body/eval_jaxpr/psum | solution.py:71
  851.8 35.5 %all-reduce.4 = f32[1024]{0:T(1024)S(1)} all-reduce(f32[1024]{0:T(1024)S(1)} %dynamic-update-slice.105), channel_id=1, replica_groups=mesh['col'=16,'tile'=16] {'tile'}, use_global_device_ids=true, to_apply=%add.1 | all-reduce | flops 1024 | bytes 8192 | tf_op jit(solution)/shard_map/while
  888.3 38.0 %psum.17 = f32[]{:T(128)} all-reduce(f32[]{:T(128)} %get-tuple-element.212), channel_id=1, replica_groups=mesh['col'=16,'tile'=16] {'tile'}, use_global_device_ids=true, to_apply=%region_21.21 | all-reduce | flops 1 | bytes 8 | tf_op jit(solution)/shard_map/while/body/eval_jaxpr/psum | solution.py:71
  933.2 35.5 %all-reduce.4 = f32[1024]{0:T(1024)S(1)} all-reduce(f32[1024]{0:T(1024)S(1)} %dynamic-update-slice.105), channel_id=1, replica_groups=mesh['col'=16,'tile'=16] {'tile'}, use_global_device_ids=true, to_apply=%add.1 | all-reduce | flops 1024 | bytes 8192 | tf_op jit(solution)/shard_map/while
  969.7 38.0 %psum.17 = f32[]{:T(128)} all-reduce(f32[]{:T(128)} %get-tuple-element.212), channel_id=1, replica_groups=mesh['col'=16,'tile'=16] {'tile'}, use_global_device_ids=true, to_apply=%region_21.21 | all-reduce | flops 1 | bytes 8 | tf_op jit(solution)/shard_map/while/body/eval_jaxpr/psum | solution.py:71
  1014.7 35.5 %all-reduce.4 = f32[1024]{0:T(1024)S(1)} all-reduce(f32[1024]{0:T(1024)S(1)} %dynamic-update-slice.105), channel_id=1, replica_groups=mesh['col'=16,'tile'=16] {'tile'}, use_global_device_ids=true, to_apply=%add.1 | all-reduce | flops 1024 | bytes 8192 | tf_op jit(solution)/shard_map/while
  1051.2 38.0 %psum.17 = f32[]{:T(128)} all-reduce(f32[]{:T(128)} %get-tuple-element.212), channel_id=1, replica_groups=mesh['col'=16,'tile'=16] {'tile'}, use_global_device_ids=true, to_apply=%region_21.21 | all-reduce | flops 1 | bytes 8 | tf_op jit(solution)/shard_map/while/body/eval_jaxpr/psum | solution.py:71
  1096.1 35.5 %all-reduce.4 = f32[1024]{0:T(1024)S(1)} all-reduce(f32[1024]{0:T(1024)S(1)} %dynamic-update-slice.105), channel_id=1, replica_groups=mesh['col'=16,'tile'=16] {'tile'}, use_global_device_ids=true, to_apply=%add.1 | all-reduce | flops 1024 | bytes 8192 | tf_op jit(solution)/shard_map/while
  1132.6 38.0 %psum.17 = f32[]{:T(128)} all-reduce(f32[]{:T(128)} %get-tuple-element.212), channel_id=1, replica_groups=mesh['col'=16,'tile'=16] {'tile'}, use_global_device_ids=true, to_apply=%region_21.21 | all-reduce | flops 1 | bytes 8 | tf_op jit(solution)/shard_map/while/body/eval_jaxpr/psum | solution.py:71
  1177.6 35.5 %all-reduce.4 = f32[1024]{0:T(1024)S(1)} all-reduce(f32[1024]{0:T(1024)S(1)} %dynamic-update-slice.105), channel_id=1, replica_groups=mesh['col'=16,'tile'=16] {'tile'}, use_global_device_ids=true, to_apply=%add.1 | all-reduce | flops 1024 | bytes 8192 | tf_op jit(solution)/shard_map/while
  1214.1 38.0 %psum.17 = f32[]{:T(128)} all-reduce(f32[]{:T(128)} %get-tuple-element.212), channel_id=1, replica_groups=mesh['col'=16,'tile'=16] {'tile'}, use_global_device_ids=true, to_apply=%region_21.21 | all-reduce | flops 1 | bytes 8 | tf_op jit(solution)/shard_map/while/body/eval_jaxpr/psum | solution.py:71
  1295.5 38.0 %psum.17 = f32[]{:T(128)} all-reduce(f32[]{:T(128)} %get-tuple-element.212), channel_id=1, replica_groups=mesh['col'=16,'tile'=16] {'tile'}, use_global_device_ids=true, to_apply=%region_21.21 | all-reduce | flops 1 | bytes 8 | tf_op jit(solution)/shard_map/while/body/eval_jaxpr/psum | solution.py:71
  1376.9 38.0 %psum.17 = f32[]{:T(128)} all-reduce(f32[]{:T(128)} %get-tuple-element.212), channel_id=1, replica_groups=mesh['col'=16,'tile'=16] {'tile'}, use_global_device_ids=true, to_apply=%region_21.21 | all-reduce | flops 1 | bytes 8 | tf_op jit(solution)/shard_map/while/body/eval_jaxpr/psum | solution.py:71
  1421.9 35.5 %all-reduce.4 = f32[1024]{0:T(1024)S(1)} all-reduce(f32[1024]{0:T(1024)S(1)} %dynamic-update-slice.105), channel_id=1, replica_groups=mesh['col'=16,'tile'=16] {'tile'}, use_global_device_ids=true, to_apply=%add.1 | all-reduce | flops 1024 | bytes 8192 | tf_op jit(solution)/shard_map/while
  1458.4 38.0 %psum.17 = f32[]{:T(128)} all-reduce(f32[]{:T(128)} %get-tuple-element.212), channel_id=1, replica_groups=mesh['col'=16,'tile'=16] {'tile'}, use_global_device_ids=true, to_apply=%region_21.21 | all-reduce | flops 1 | bytes 8 | tf_op jit(solution)/shard_map/while/body/eval_jaxpr/psum | solution.py:71
  1503.4 35.5 %all-reduce.4 = f32[1024]{0:T(1024)S(1)} all-reduce(f32[1024]{0:T(1024)S(1)} %dynamic-update-slice.105), channel_id=1, replica_groups=mesh['col'=16,'tile'=16] {'tile'}, use_global_device_ids=true, to_apply=%add.1 | all-reduce | flops 1024 | bytes 8192 | tf_op jit(solution)/shard_map/while
  1539.8 38.0 %psum.17 = f32[]{:T(128)} all-reduce(f32[]{:T(128)} %get-tuple-element.212), channel_id=1, replica_groups=mesh['col'=16,'tile'=16] {'tile'}, use_global_device_ids=true, to_apply=%region_21.21 | all-reduce | flops 1 | bytes 8 | tf_op jit(solution)/shard_map/while/body/eval_jaxpr/psum | solution.py:71
  1584.8 35.5 %all-reduce.4 = f32[1024]{0:T(1024)S(1)} all-reduce(f32[1024]{0:T(1024)S(1)} %dynamic-update-slice.105), channel_id=1, replica_groups=mesh['col'=16,'tile'=16] {'tile'}, use_global_device_ids=true, to_apply=%add.1 | all-reduce | flops 1024 | bytes 8192 | tf_op jit(solution)/shard_map/while
  1621.3 38.0 %psum.17 = f32[]{:T(128)} all-reduce(f32[]{:T(128)} %get-tuple-element.212), channel_id=1, replica_groups=mesh['col'=16,'tile'=16] {'tile'}, use_global_device_ids=true, to_apply=%region_21.21 | all-reduce | flops 1 | bytes 8 | tf_op jit(solution)/shard_map/while/body/eval_jaxpr/psum | solution.py:71
  1666.3 35.5 %all-reduce.4 = f32[1024]{0:T(1024)S(1)} all-reduce(f32[1024]{0:T(1024)S(1)} %dynamic-update-slice.105), channel_id=1, replica_groups=mesh['col'=16,'tile'=16] {'tile'}, use_global_device_ids=true, to_apply=%add.1 | all-reduce | flops 1024 | bytes 8192 | tf_op jit(solution)/shard_map/while
  1702.7 38.0 %psum.17 = f32[]{:T(128)} all-reduce(f32[]{:T(128)} %get-tuple-element.212), channel_id=1, replica_groups=mesh['col'=16,'tile'=16] {'tile'}, use_global_device_ids=true, to_apply=%region_21.21 | all-reduce | flops 1 | bytes 8 | tf_op jit(solution)/shard_map/while/body/eval_jaxpr/psum | solution.py:71
  1784.2 38.0 %psum.17 = f32[]{:T(128)} all-reduce(f32[]{:T(128)} %get-tuple-element.212), channel_id=1, replica_groups=mesh['col'=16,'tile'=16] {'tile'}, use_global_device_ids=true, to_apply=%region_21.21 | all-reduce | flops 1 | bytes 8 | tf_op jit(solution)/shard_map/while/body/eval_jaxpr/psum | solution.py:71
  1865.6 38.0 %psum.17 = f32[]{:T(128)} all-reduce(f32[]{:T(128)} %get-tuple-element.212), channel_id=1, replica_groups=mesh['col'=16,'tile'=16] {'tile'}, use_global_device_ids=true, to_apply=%region_21.21 | all-reduce | flops 1 | bytes 8 | tf_op jit(solution)/shard_map/while/body/eval_jaxpr/psum | solution.py:71
  1947.1 38.0 %psum.17 = f32[]{:T(128)} all-reduce(f32[]{:T(128)} %get-tuple-element.212), channel_id=1, replica_groups=mesh['col'=16,'tile'=16] {'tile'}, use_global_device_ids=true, to_apply=%region_21.21 | all-reduce | flops 1 | bytes 8 | tf_op jit(solution)/shard_map/while/body/eval_jaxpr/psum | solution.py:71
  2028.5 38.0 %psum.17 = f32[]{:T(128)} all-reduce(f32[]{:T(128)} %get-tuple-element.212), channel_id=1, replica_groups=mesh['col'=16,'tile'=16] {'tile'}, use_global_device_ids=true, to_apply=%region_21.21 | all-reduce | flops 1 | bytes 8 | tf_op jit(solution)/shard_map/while/body/eval_jaxpr/psum | solution.py:71
  (341 shorter events, 657.9 us)
Async XLA Ops:
  7.2 0.8 copy-start
  7.2 54.4 %all-gather.6.cloned.1.call-start = ((), (), s32[]{:S(2)}) async-start(), calls=%async_computation.4 | async-start | bytes 2228224 | tf_op jit(solution)/shard_map/all_gather | solution.py:29
  7.9 175.1 %all-reduce.7.cloned.1.call-start = ((), (), s32[]{:S(2)}) async-start(), calls=%async_computation.1 | async-start | bytes 8388608 | tf_op jit(solution)/shard_map/psum | solution.py:35
  69.5 546.9 %all-gather.4.cloned.1.call-start = ((), (), s32[]{:S(2)}) async-start(), calls=%async_computation.2 | async-start | bytes 8912896 | tf_op jit(solution)/shard_map/all_gather | solution.py:45
  197.8 1.9 copy-start.3
  247.7 2.0 copy-start.2
  521.0 18.8 copy-start.5
  523.1 17.6 copy-start.7
  523.1 93.3 %copy-start.4 = (bf16[1,64,4,1024]{3,2,1,0:T(4,128)(2,1)S(1)}, bf16[1,64,4,1024]{3,2,1,0:T(4,128)(2,1)}, u32[]{:S(2)}) copy-start(bf16[1,64,4,1024]{3,2,1,0:T(4,128)(2,1)} %param.9) | copy-start | bytes 1572868
  528.1 11.7 collective-permute-start.1
  540.7 216.8 %reduce-scatter.2.cloned.1.call-start = ((), (), s32[]{:S(2)}) async-start(), calls=%async_computation.3 | async-start | bytes 17825792 | tf_op jit(solution)/shard_map/reduce_scatter | solution.py:51
  642.2 116.6 %copy-start.8 = (f32[1,4]{1,0:T(1,128)S(1)}, f32[1,4]{1,0:T(1,128)}, u32[]{:S(2)}) copy-start(f32[1,4]{1,0:T(1,128)} %param.14) | copy-start | bytes 52
  642.2 120.2 %copy-start.6 = (f32[1024]{0:T(1024)S(1)}, f32[1024]{0:T(1024)}, u32[]{:S(2)}) copy-start(f32[1024]{0:T(1024)} %param.15) | copy-start | bytes 12292
  642.2 120.2 %copy-start.9 = (u32[256]{0:T(256)S(1)}, u32[256]{0:T(256)}, u32[]{:S(2)}) copy-start(u32[256]{0:T(256)} %constant.448) | copy-start | bytes 3076
  642.2 1425.5 %copy-start.1 = (bf16[1,4,4,1024]{3,2,1,0:T(4,128)(2,1)S(1)}, bf16[1,4,4,1024]{3,2,1,0:T(4,128)(2,1)}, u32[]{:S(2)}) copy-start(bf16[1,4,4,1024]{3,2,1,0:T(4,128)(2,1)} %param.12) | copy-start | bytes 98308
  762.4 6.1 collective-permute-start
  845.5 6.1 collective-permute-start
  927.0 6.1 collective-permute-start
  1008.4 6.1 collective-permute-start
  1089.8 6.1 collective-permute-start
  1171.3 6.1 collective-permute-start
  1252.7 6.1 collective-permute-start
  1334.2 6.1 collective-permute-start
  1415.6 6.1 collective-permute-start
  1497.1 6.1 collective-permute-start
  1578.5 6.1 collective-permute-start
  1660.0 6.1 collective-permute-start
  1741.4 6.1 collective-permute-start
  1822.9 6.1 collective-permute-start
  1904.3 6.1 collective-permute-start
  1985.8 6.1 collective-permute-start
  2067.2 0.5 copy-start.10
Sparse Core Ops, SparseCore 0:
  10.4 51.0 all-gather.5
  69.7 113.3 all-reduce.6
  540.8 75.6 all-gather.3
  642.3 115.1 reduce-scatter.1
where the time goes:
time: 2080 us; the launch traced here: 2070 us
  blocking collectives  1180 us (57%)
  waiting for transfers between devices  411 us (20%)
  other arithmetic  264 us (13%)
  matrix products  91.5 us (4%)
  local copies, waits for them, and re-layouts  56 us (3%)
  starting transfers between devices  32.8 us (2%)
  loops' own time  21.8 us (1%)
    psum x16, blocking collectives, relay_split(): squares = lax.psum(jnp.sum(weighted * weighted), 'tile')  609 us
    while x16, blocking collectives  568 us
    another operation x30, other arithmetic, local(): lower_factor = jnp.linalg.cholesky(gram_total)  167 us
    reduce_scatter x1, waiting for transfers between devices, local(): lax.psum_scatter(jnp.einsum('cdbr,brk->kdc', left_absorbed, matching, pre...  115 us
    psum x1, waiting for transfers between devices, local(): lax.psum(gram_local, 'tile')  112 us
    another operation x3, other arithmetic, local(): jax.scipy.linalg.solve_triangular(lower_factor, range_flat.T, lower=True)  83.6 us
    all_gather x1, waiting for transfers between devices, local(): lax.all_gather(left_basis, 'tile', axis=0, tiled=True)  75.5 us
    ppermute x17, waiting for transfers between devices, passed_along(): return lax.ppermute(block, axis, route)  54.7 us
  transfers between devices with their start and end apart: 21, of which 21 were waited for; matrix products, arithmetic and copies ran while one was open for 1% of the time, Pallas kernels for 0%

commit v1 on v0

v1 whole, which is shorter than its diff:
```python
import functools

import jax
import jax.numpy as jnp
from jax import lax
from jax.experimental import pallas as pl
from jax.experimental.pallas import tpu as pltpu
from jax.sharding import PartitionSpec as P

GRAM_SHIFT = 0.001
NB = 128
OWNER = 0
HIGHEST = lax.Precision.HIGHEST
MESH = pl.DeviceIdType.MESH
VMEM = pl.BlockSpec(memory_space=pltpu.VMEM)


def f32_dot(x, y, dims=(((1,), (0,)), ((), ()))):
    return lax.dot_general(x, y, dims, precision=HIGHEST, preferred_element_type=jnp.float32)


def factor_block(block, inv_ref):
    sub = lax.broadcasted_iota(jnp.int32, (8, NB), 0)
    lane = lax.broadcasted_iota(jnp.int32, (8, NB), 1)
    a0 = tuple(block[8 * i:8 * i + 8, :] for i in range(16))
    m0 = tuple((lane == sub + 8 * i).astype(jnp.float32) for i in range(16))

    def along(x, t):
        return jnp.broadcast_to(x[:, t:t + 1], (8, NB))

    def down(x, t):
        return jnp.broadcast_to(x[t:t + 1, :], (8, NB))

    def tree(terms):
        while len(terms) > 1:
            terms = [terms[i] + terms[i + 1] for i in range(0, len(terms), 2)]
        return terms[0]

    def group(count, g, carry):
        a, m = list(carry[0]), list(carry[1])
        p, n = a[0], m[0]
        c = [along(p, t) for t in range(8)]
        done = jnp.zeros((8, NB), jnp.float32)
        for s in range(8):
            here = sub == s
            pivot = down(c[s], s)
            inv = 1.0 / pivot
            nrow = down(n, s)
            done = jnp.where(here, nrow * lax.rsqrt(pivot), done)
            column = c[s]

            def step(x, row):
                row = row * inv
                return jnp.where(here, row, x - column * row)

            for t in range(s + 1, 8):
                c[t] = step(c[t], down(c[t], s))
            p = step(p, down(p, s))
            n = step(n, nrow)
        inv_ref[pl.ds(pl.multiple_of(g * 8, 8), 8), :] = done
        prow = [down(p, t) for t in range(8)]
        nrow = [down(n, t) for t in range(8)]
        for i in range(1, count):
            x = [along(a[i], t) for t in range(8)]
            a[i] = a[i] - tree([x[t] * prow[t] for t in range(8)])
            m[i] = m[i] - tree([x[t] * nrow[t] for t in range(8)])
        zero = jnp.zeros((8, NB), jnp.float32)
        return tuple(pltpu.roll(x, NB - 8, 1) for x in a[1:]) + (zero,), tuple(m[1:]) + (zero,)

    carry = (a0, m0)
    for lo in range(0, 16, 4):
        carry = (carry[0][:16 - lo], carry[1][:16 - lo])
        carry = lax.fori_loop(lo, lo + 4, functools.partial(group, 16 - lo), carry)


def basis_kernel(g_ref, r_ref, q_ref, s_ref, x_ref, inv_ref):
    n = g_ref.shape[0]
    eye = lax.broadcasted_iota(jnp.int32, (NB, NB), 0) == lax.broadcasted_iota(jnp.int32, (NB, NB), 1)
    for o in range(0, n, NB):
        e = o + NB
        src, rows = (g_ref, r_ref) if o == 0 else (s_ref, x_ref)
        factor_block(src[o:e, o:e] + jnp.where(eye, GRAM_SHIFT, 0.0), inv_ref)
        inv = inv_ref[...]
        q = f32_dot(rows[:, o:e], inv, (((1,), (1,)), ((), ())))
        q_ref[:, o:e] = q.astype(q_ref.dtype)
        if e == n:
            break
        upper = f32_dot(inv, src[o:e, e:])
        x_ref[:, e:] = rows[:, e:] - f32_dot(q, upper)
        for i in range(e, n, NB):
            s_ref[i:i + NB, i:] = src[i:i + NB, i:] - f32_dot(upper[:, i - e:i - e + NB].T, upper[:, i - e:])


def basis_of(gram, rows):
    n = gram.shape[0]
    return pl.pallas_call(
        basis_kernel,
        out_shape=jax.ShapeDtypeStruct(rows.shape, jnp.bfloat16),
        in_specs=[VMEM] * 2,
        out_specs=VMEM,
        scratch_shapes=[
            pltpu.VMEM((n, n), jnp.float32),
            pltpu.VMEM(rows.shape, jnp.float32),
            pltpu.VMEM((NB, NB), jnp.float32),
        ],
        compiler_params=pltpu.CompilerParams(vmem_limit_bytes=40 << 20),
        cost_estimate=pl.CostEstimate(flops=6 * 10**10, bytes_accessed=6 << 20, transcendentals=0),
    )(gram, rows)


def relay_kernel(cols, tiles, t_ref, edge_ref, env_ref, tall, across, arrived, stage, landed,
                 gather_send, gather_recv, chain_send, chain_recv, spread_send, spread_recv):
    col = lax.axis_index("col")
    tile = lax.axis_index("tile")
    share, width = t_ref.shape
    owner = tile == OWNER
    barrier = pltpu.get_barrier_semaphore()
    others = [t for t in range(tiles) if t != OWNER]

    def gather(slot, where):
        return pltpu.make_async_remote_copy(
            src_ref=t_ref, dst_ref=tall.at[slot], send_sem=gather_send, recv_sem=gather_recv.at[slot],
            device_id={"tile": where}, device_id_type=MESH)

    def spread(where):
        return pltpu.make_async_remote_copy(
            src_ref=stage, dst_ref=landed, send_sem=spread_send.at[where], recv_sem=spread_recv,
            device_id={"tile": where}, device_id_type=MESH)

    def chain(where):
        return pltpu.make_async_remote_copy(
            src_ref=stage, dst_ref=arrived, send_sem=chain_send, recv_sem=chain_recv,
            device_id={"col": where}, device_id_type=MESH)

    @pl.when(jnp.logical_not(owner))
    def _():
        pl.semaphore_signal(barrier, inc=1, device_id={"tile": OWNER}, device_id_type=MESH)
        pl.semaphore_wait(barrier, 1)
        gather(tile, OWNER).start()
        gather(tile, OWNER).wait_send()
        spread(OWNER).wait_recv()
        env_ref[...] = landed[...]

    @pl.when(owner)
    def _():
        for t in others:
            pl.semaphore_signal(barrier, inc=1, device_id={"tile": t}, device_id_type=MESH)

        for step in (1, cols - 1):
            pl.semaphore_signal(barrier, inc=1, device_id={"col": (col + step) % cols}, device_id_type=MESH)
        pl.semaphore_wait(barrier, len(others) + 2)
        tall[OWNER] = t_ref[...]
        per = NB // share
        for block in range(tiles // per):
            for t in range(block * per, block * per + per):
                if t != OWNER:
                    gather(t, t).wait_recv()
            rows = tall[block * per:block * per + per].reshape(NB, width).astype(jnp.float32)
            across[:, block * NB:block * NB + NB] = rows.T.astype(jnp.bfloat16)

        @pl.when(col == 0)
        def _():
            arrived[...] = edge_ref[...]

        @pl.when(col > 0)
        def _():
            chain(col).wait_recv()

        env = arrived[...]
        high = env.astype(jnp.bfloat16).astype(jnp.float32)
        middle = (env - high).astype(jnp.bfloat16).astype(jnp.float32)
        low = env - high - middle
        row = lax.broadcasted_iota(jnp.int32, (8, width), 0)
        parts = jnp.where(row == 0, high, jnp.where(row == 1, middle, jnp.where(row == 2, low, 0.0)))
        product = jnp.dot(parts.astype(jnp.bfloat16), across[...], preferred_element_type=jnp.float32)
        weighted = jnp.sum(product, axis=0, keepdims=True)
        squares = jnp.sum(weighted * weighted, axis=1, keepdims=True)
        stage[...] = weighted * (jnp.sqrt(jnp.float32(width)) / jnp.sqrt(squares + 1e-06))

        @pl.when(col < cols - 1)
        def _():
            chain(col + 1).start()

        for t in others:
            spread(t).start()
        env_ref[...] = stage[...]
        for t in others:
            spread(t).wait_send()

        @pl.when(col < cols - 1)
        def _():
            chain(col + 1).wait_send()


def relay(transfer_rows, left_edge, cols, tiles):
    share, width = transfer_rows.shape
    row = jax.ShapeDtypeStruct((1, width), jnp.float32)
    return pl.pallas_call(
        functools.partial(relay_kernel, cols, tiles),
        out_shape=row,
        in_specs=[VMEM] * 2,
        out_specs=VMEM,
        scratch_shapes=[
            pltpu.VMEM((tiles, share, width), jnp.bfloat16),
            pltpu.VMEM((width, width), jnp.bfloat16),
            pltpu.VMEM((1, width), jnp.float32),
            pltpu.VMEM((1, width), jnp.float32),
            pltpu.VMEM((1, width), jnp.float32),
            pltpu.SemaphoreType.DMA,
            pltpu.SemaphoreType.DMA((tiles,)),
            pltpu.SemaphoreType.DMA,
            pltpu.SemaphoreType.DMA,
            pltpu.SemaphoreType.DMA((tiles,)),
            pltpu.SemaphoreType.DMA,
        ],
        compiler_params=pltpu.CompilerParams(collective_id=1, has_side_effects=True, vmem_limit_bytes=32 << 20),
    )(transfer_rows, left_edge.reshape(1, width))


def passed_along(block, axis, distance):
    devices = range(lax.axis_size(axis))
    route = [(i - distance, i) for i in devices if i - distance in devices]
    return lax.ppermute(block, axis, route)


def local(boundary, row_tensors, sketch_bond, sketch_phys, edge_factor, closing, left_edge):
    highest = lax.Precision.HIGHEST
    own_site = boundary[0]
    row_tensor = row_tensors[0].astype(jnp.float32)
    bond_sketch = sketch_bond[0]
    phys_map = jnp.einsum(
        "lurd,ldk->urk", row_tensor, sketch_phys[0].astype(jnp.float32), precision=highest
    )
    local_rows, legs, width = own_site.shape
    sketched = jnp.einsum(
        "bua,ka->buk",
        own_site,
        lax.all_gather(bond_sketch, "tile", axis=0, tiled=True),
        preferred_element_type=jnp.float32,
    )
    range_rows = jnp.sum(sketched[:, :, None, :] * phys_map[None], axis=1)
    range_flat = range_rows.reshape(local_rows * legs, width)
    gram_local = jnp.dot(range_flat.T, range_flat, precision=highest)
    gram_total = lax.psum(gram_local, "tile")
    basis = basis_of(gram_total, range_flat).reshape(local_rows, legs, width)
    arrived = passed_along(basis, "col", 1)
    first_column = lax.axis_index("col") == 0
    left_basis = jnp.where(first_column, edge_factor, arrived)
    left_part = jnp.einsum(
        "alc,bua->club",
        lax.all_gather(left_basis, "tile", axis=0, tiled=True),
        own_site,
        preferred_element_type=jnp.float32,
    )
    left_absorbed = jnp.einsum("club,lurd->cdbr", left_part, row_tensor, precision=highest)
    new_site = lax.psum_scatter(
        jnp.einsum("cdbr,brk->kdc", left_absorbed, basis.astype(jnp.float32), precision=highest),
        "tile",
        scatter_dimension=0,
        tiled=True,
    )
    new_site = new_site.astype(jnp.bfloat16)
    transfer_rows = jnp.einsum(
        "kdc,d->kc", new_site.astype(jnp.float32), closing[0], precision=highest
    ).astype(jnp.bfloat16)
    env = relay(transfer_rows, left_edge, lax.axis_size("col"), lax.axis_size("tile"))
    share = transfer_rows.shape[0]
    env_local = lax.dynamic_slice(env, (0, lax.axis_index("tile") * share), (1, share))
    return (new_site[None], env_local)


def solution(mesh):
    in_specs = (
        P("col", "tile", None, None),
        P("col", None, None, None, None),
        P("col", "tile", None),
        P("col", None, None, None),
        P("tile", None, None),
        P("col", None),
        P(),
    )
    out_specs = (P("col", "tile", None, None), P("col", "tile"))
    return jax.shard_map(local, mesh=mesh, in_specs=in_specs, out_specs=out_specs, check_vma=False)
```

time: 2080 us -> 541 us (0.26)
  the two profiles are of different devices: /device:TPU:130 before, /device:TPU:229 now
where the time goes in v1:
time: 541 us; the launch traced here: 537 us
  waiting for transfers between devices  366 us (68%)
  Pallas kernels  110 us (20%)
  matrix products  35.6 us (7%)
  between operations  14.4 us (3%)
  local copies, waits for them, and re-layouts  5.5 us (1%)
    reduce_scatter x1, waiting for transfers between devices, local(): lax.psum_scatter(jnp.einsum('cdbr,brk->kdc', left_absorbed, basis.astype(...  115 us
    psum x1, waiting for transfers between devices, local(): gram_total = lax.psum(gram_local, 'tile')  115 us
    all_gather x1, waiting for transfers between devices, local(): lax.all_gather(left_basis, 'tile', axis=0, tiled=True)  83.1 us
    pallas_call x1, Pallas kernels, relay(): pl.pallas_call(functools.partial(relay_kernel, cols, tiles), out_shape=ro...  57.9 us
    pallas_call x1, Pallas kernels, basis_of(): pl.pallas_call(basis_kernel, out_shape=jax.ShapeDtypeStruct(rows.shape, j...  52.5 us
    all_gather x1, waiting for transfers between devices, local(): lax.all_gather(bond_sketch, 'tile', axis=0, tiled=True)  48.6 us
    dot_general x1, matrix products, local(): jnp.einsum('cdbr,brk->kdc', left_absorbed, basis.astype(jnp.float32), pre...  11.7 us
  transfers between devices with their start and end apart: 5, of which 5 were waited for; matrix products, arithmetic and copies ran while one was open for 0% of the time, Pallas kernels for 0%

profile of v1, /device:TPU:229, one launch (start us, length us, event | category | flops | bytes accessed | tf_op | source)
XLA Modules:
  0.0 536.5 jit_solution(16189040915591977640)
XLA Ops:
  7.2 0.0 all-gather.6.cloned.1.call-start
  7.2 0.7 all-gather.6.cloned.1.call-update
  7.9 0.0 all-reduce.2.cloned.1.call-start
  8.0 1.2 convolution_bitcast_fusion.2
  9.1 48.6 %all-gather.6.cloned.1.call-done = bf16[1,1024,1024]{2,1,0:T(8,128)(2,1)} async-done(((bf16[1,64,1024]{2,1,0:T(8,128)(2,1)}), bf16[1,1024,1024]{2,1,0:T(8,128)(2,1)}) %all-gather.6.cloned.1.call-update) | async-done | bytes 2097168 | tf_op jit(solution)/shard_map/all_gather | solution.py:238
  57.8 2.5 fusion.11
  60.3 0.3 multiply_reduce_fusion
  60.6 5.1 convolution_bitcast_fusion.1
  65.7 0.0 all-reduce.2.cloned.1.call-update
  65.7 0.0 all-gather.4.cloned.1.call-start
  65.7 0.7 copy.24
  66.4 0.4 reshape.15.r_ref
  66.8 114.9 %all-reduce.2.cloned.1.call-done.g_ref = f32[1024,1024]{1,0:T(8,128)} async-done(((f32[1024,1024]{1,0:T(8,128)}), f32[1024,1024]{1,0:T(8,128)}) %all-reduce.2.cloned.1.call-update) | async-done | bytes 4194320 | tf_op jit(solution)/shard_map/psum | solution.py:244
  181.7 2.2 copy-done.2
  183.9 52.5 %shard_map.86 = bf16[256,1024]{1,0:T(8,128)(2,1)S(1)} custom-call(f32[1024,1024]{1,0:T(8,128)S(1)} %copy-done.2, f32[256,1024]{1,0:T(8,128)S(1)} %reshape.15.r_ref), custom_call_target="tpu_custom_call" | custom-call | flops 60000002048 | bytes 6291456 | tf_op jit(solution)/shard_map/pallas_call | solution.py:96
  236.4 0.2 reshape.16
  236.6 1.3 collective-permute-start
  237.9 2.8 collective-permute-done
  240.7 0.8 broadcast_select_fusion
  241.6 0.0 reduce-scatter.2.cloned.1.call-start
  241.7 0.2 copy.28
  241.9 83.1 %all-gather.4.cloned.1.call-done = bf16[1024,4,1024]{2,1,0:T(4,128)(2,1)} async-done(((bf16[64,4,1024]{2,1,0:T(4,128)(2,1)}), bf16[1024,4,1024]{2,1,0:T(4,128)(2,1)}) %all-gather.4.cloned.1.call-update) | async-done | bytes 8388624 | tf_op jit(solution)/shard_map/all_gather | solution.py:251
  325.0 7.4 %fusion.8 = f32[1024,4,4,64,1]{0,3,2,1,4:T(8,128)S(1)} fusion(bf16[1024,4,1024,1]{2,1,0,3:T(4,128)(2,1)} %bitcast.66, bf16[64,4,1024]{2,1,0:T(4,128)(2,1)S(1)} %bitcast.62), kind=kOutput, calls=%fused_computation.8 | convolution fusion | flops 2147483648 | bytes 13107200 | tf_op jit(solution)/shard_map/alc,bua->club/dot_general | solution.py:249
  332.4 6.6 %fusion.5 = f32[1024,4,64,4]{0,1,3,2:T(4,128)S(1)} fusion(f32[1024,4,4,64,1]{0,3,2,1,4:T(8,128)S(1)} %fusion.8, bf16[4,4,4,4]{1,3,0,2:T(4,128)(2,1)S(1)} %copy.28), kind=kOutput, calls=%fused_computation.7 | convolution fusion | flops 201326592 | bytes 8389120 | tf_op jit(solution)/shard_map/club,lurd->cdbr/dot_general | solution.py:255
  339.0 11.7 %convolution_bitcast_fusion = f32[1024,4,1024]{2,0,1:T(8,128)} fusion(f32[1024,4,64,4]{0,1,3,2:T(4,128)S(1)} %fusion.5, bf16[64,4,1024]{2,1,0:T(4,128)(2,1)S(1)} %reshape.16), kind=kOutput, calls=%fused_computation | convolution fusion | flops 12884901888 | bytes 21495808 | tf_op jit(solution)/shard_map/cdbr,brk->kdc/dot_general | solution.py:257
  350.8 115.4 %reduce-scatter.2.cloned.1.call-done = f32[64,4,1024]{2,0,1:T(8,128)} async-done(((f32[1024,4,1024]{2,0,1:T(8,128)}), f32[64,4,1024]{2,0,1:T(8,128)}) %reduce-scatter.2.cloned.1.call-update) | async-done | bytes 1048592 | tf_op jit(solution)/shard_map/reduce_scatter | solution.py:256
  466.1 1.3 convert_element_type.4
  467.4 1.1 fusion.16
  468.6 1.3 convert_bitcast_fusion
  469.9 1.2 copy.31
  471.1 57.9 %shard_map.87 = f32[1,1024]{1,0:T(1,128)S(1)} custom-call(bf16[64,1024]{1,0:T(8,128)(2,1)S(1)} %bitcast.58, f32[1,1024]{1,0:T(1,128)S(1)} %bitcast.59), custom_call_target="tpu_custom_call" | custom-call | tf_op jit(solution)/shard_map/pallas_call | solution.py:198
  529.0 0.6 constant_dynamic-slice_fusion
  (16 shorter events, 0.1 us)
Async XLA Ops:
  7.2 0.8 copy-start
  7.2 50.6 %all-gather.6.cloned.1.call-start = ((), (), s32[]{:S(2)}) async-start(), calls=%async_computation.4 | async-start | bytes 2228224 | tf_op jit(solution)/shard_map/all_gather | solution.py:238
  7.9 173.8 %all-reduce.2.cloned.1.call-start = ((), (), s32[]{:S(2)}) async-start(), calls=%async_computation.1 | async-start | bytes 8388608 | tf_op jit(solution)/shard_map/psum | solution.py:244
  65.7 259.3 %all-gather.4.cloned.1.call-start = ((), (), s32[]{:S(2)}) async-start(), calls=%async_computation.2 | async-start | bytes 8912896 | tf_op jit(solution)/shard_map/all_gather | solution.py:251
  181.7 2.2 copy-start.2
  183.9 56.8 %copy-start.4 = (bf16[64,4,1024]{2,1,0:T(4,128)(2,1)S(1)}, bf16[64,4,1024]{2,1,0:T(4,128)(2,1)}, u32[]{:S(2)}) copy-start(bf16[64,4,1024]{2,1,0:T(4,128)(2,1)} %param.11) | copy-start | bytes 1572868
  183.9 57.8 %copy-start.5 = (bf16[1,4,4,4,4]{4,3,2,1,0:T(4,128)(2,1)S(1)}, bf16[1,4,4,4,4]{4,3,2,1,0:T(4,128)(2,1)}, u32[]{:S(2)}) copy-start(bf16[1,4,4,4,4]{4,3,2,1,0:T(4,128)(2,1)} %param.8) | copy-start | bytes 1540
  183.9 141.0 %copy-start.3 = (bf16[1,64,4,1024]{3,2,1,0:T(4,128)(2,1)S(1)}, bf16[1,64,4,1024]{3,2,1,0:T(4,128)(2,1)}, u32[]{:S(2)}) copy-start(bf16[1,64,4,1024]{3,2,1,0:T(4,128)(2,1)} %param.7) | copy-start | bytes 1572868
  236.6 4.1 collective-permute-start
  241.6 224.5 %reduce-scatter.2.cloned.1.call-start = ((), (), s32[]{:S(2)}) async-start(), calls=%async_computation.3 | async-start | bytes 17825792 | tf_op jit(solution)/shard_map/reduce_scatter | solution.py:256
  350.7 116.7 %copy-start.6 = (f32[1,4]{1,0:T(1,128)S(1)}, f32[1,4]{1,0:T(1,128)}, u32[]{:S(2)}) copy-start(f32[1,4]{1,0:T(1,128)} %param.12) | copy-start | bytes 52
  350.7 120.3 %copy-start.1 = (f32[1024]{0:T(1024)S(1)}, f32[1024]{0:T(1024)}, u32[]{:S(2)}) copy-start(f32[1024]{0:T(1024)} %param.13) | copy-start | bytes 12292
Sparse Core Ops, SparseCore 0:
  10.4 47.2 all-gather.5
  65.8 115.8 all-reduce.1
  241.7 83.1 all-gather.3
  350.9 115.2 reduce-scatter.1
